TPU v7x, 128 devices: a whole 4x4x4 slice. The times are simulated.
128 devices in a mesh: row: 8 (over x, core), col: 16 (over y, z).
Axes of the slice: x: 4, y: 4, z: 4, core: 2. Of those that a mesh axis runs over, the one named last changes fastest.
Arguments:
- coupling: bfloat16 [128, 4096, 1024], P(('row', 'col')), may hold values from -0.09375 to 0.09375
- modes: bfloat16 [128, 200, 4096], P(('row', 'col')), may hold values from -6 to 6
- flexibility: float32 [128, 200], P(('row', 'col')), may hold values from 0.002 to 0.02
- widths: int32 [128], P(('row', 'col')), may hold values from 512 to 1024
- segments: int32 [128, 8], replicated, may hold values from 0 to 95, as said below
Outputs:
- interface: float32 [12288, 12288], P('row', 'col')
Inputs may be any that keep to these rules, and one draw needn't show every extreme that they name: `segments`: the 8 segment numbers of a substructure are distinct, and modulo 16 they are 8 cyclically consecutive residues. `widths`: columns at and beyond a substructure's width are padding.
All inputs are finite; a program needn't handle non-finite values.
Results may differ from a plain program's by a relative error of at most 0.0003.
Values sent between devices are 32-bit elements; how exact they have to be, the bound alone decides.
A program may use at most 192 MiB of HBM per device.

v0:
```python
import functools

import jax
import jax.numpy as jnp
from jax import lax
from jax.sharding import Mesh
from jax.sharding import PartitionSpec as P

TILE = 128
NG = 12288
ROW = ("row_0", "row_1")
COL = ("col_0", "col_1")
ROW_COL = ("row_0", "row_1", "col_0", "col_1")


def by_axis(shard, axes):
    return functools.reduce(lax.psum, axes, shard)


def substructure_block(factor, modal_rows, weights, width):
    padded = factor.shape[1]
    columns = lax.broadcasted_iota(jnp.int32, (1, padded), 1)
    masked = jnp.where(columns < width, factor, jnp.zeros((), factor.dtype))
    static = lax.dot_general(
        masked, masked, (((0,), (0,)), ((), ())), preferred_element_type=jnp.float32
    )
    projected = jnp.dot(modal_rows, masked, preferred_element_type=jnp.float32)
    modal = lax.dot_general(
        projected * weights[:, None],
        projected,
        (((0,), (0,)), ((), ())),
        precision=lax.Precision.HIGHEST,
        preferred_element_type=jnp.float32,
    )
    return static - modal


def rank_among(residue_class):
    count = residue_class.shape[-1]
    places = lax.broadcasted_iota(jnp.int32, (count, count), 0)
    others = lax.broadcasted_iota(jnp.int32, (count, count), 1)
    same = residue_class[..., :, None] == residue_class[..., None, :]
    return jnp.sum(jnp.where(same & (others < places), 1, 0), axis=-1).astype(jnp.int32)


def body(coupling, modes, flexibility, widths, segments):
    row_count = lax.axis_size(ROW)
    col_count = lax.axis_size(COL)
    device_total = row_count * col_count
    local_subs = coupling.shape[0]
    seg_count = coupling.shape[2] // TILE
    seg_total = NG // TILE
    row_tiles = seg_total // row_count
    col_tiles = seg_total // col_count
    row_cap = -(-seg_count // row_count)
    col_cap = -(-seg_count // col_count)
    member_cap = row_cap * col_cap
    capacity = local_subs * member_cap
    slots_all = device_total * capacity
    my_row = lax.axis_index(ROW)
    my_col = lax.axis_index(COL)
    device_id = my_row * col_count + my_col
    blocks = jnp.stack(
        [
            substructure_block(coupling[0], modes[0], flexibility[0], widths[0]).reshape(
                seg_count, TILE, seg_count, TILE
            )
        ]
    )
    mine = lax.dynamic_slice_in_dim(segments, device_id * local_subs, local_subs, 0)
    own_diag = jnp.stack(
        [
            jnp.diagonal(blocks[:, index, :, index, :], axis1=1, axis2=2)
            for index in range(seg_count)
        ],
        axis=1,
    )
    seg_range = lax.broadcasted_iota(jnp.int32, (1, seg_total), 1)
    seg_hot = jnp.where(mine.reshape(-1)[:, None] == seg_range, 1.0, 0.0).astype(jnp.float32)
    partial_diag = lax.dot_general(
        seg_hot,
        own_diag.reshape(local_subs * seg_count, TILE),
        (((0,), (0,)), ((), ())),
        precision=lax.Precision.HIGHEST,
        preferred_element_type=jnp.float32,
    )
    summed_diag = by_axis(partial_diag, ROW_COL)
    row_diag = lax.dynamic_index_in_dim(
        summed_diag.reshape(row_tiles, row_count, TILE), my_row, 1, keepdims=False
    )
    col_diag = lax.dynamic_index_in_dim(
        summed_diag.reshape(col_tiles, col_count, TILE), my_col, 1, keepdims=False
    )
    row_res = mine % row_count
    col_res = mine % col_count
    row_rank = rank_among(row_res)
    col_rank = rank_among(col_res)
    member_ids = lax.broadcasted_iota(jnp.int32, (local_subs, seg_count, seg_count), 0)
    target = (
        (row_res[:, :, None] * col_count + col_res[:, None, :]) * capacity
        + member_ids * member_cap
        + row_rank[:, :, None] * col_cap
        + col_rank[:, None, :]
    )
    flat_target = target.reshape(-1)
    slot_ids = lax.broadcasted_iota(jnp.int32, (slots_all, flat_target.shape[0]), 0)
    matches = flat_target[None, :] == slot_ids
    tile_ids = lax.broadcasted_iota(jnp.int32, matches.shape, 1)
    source = jnp.sum(jnp.where(matches, tile_ids, 0), axis=1)
    filled = jnp.any(matches, axis=1)
    per_member = seg_count * seg_count
    member_src = source // per_member
    row_src = source % per_member // seg_count
    col_src = source % seg_count
    outgoing = blocks[member_src, row_src, :, col_src, :]
    outgoing = jnp.where(filled[:, None, None], outgoing, jnp.zeros((), jnp.float32))
    arriving = lax.all_to_all(outgoing, ROW_COL, split_axis=0, concat_axis=0, tiled=True)
    every_row = segments % row_count
    every_col = segments % col_count
    every_row_rank = rank_among(every_row)
    every_col_rank = rank_among(every_col)
    subs_total = segments.shape[0]
    sub_ids = lax.broadcasted_iota(jnp.int32, (subs_total, seg_count, seg_count), 0)
    keeping = (every_row[:, :, None] == my_row) & (every_col[:, None, :] == my_col)
    placing = (
        sub_ids // local_subs * capacity
        + sub_ids % local_subs * member_cap
        + every_row_rank[:, :, None] * col_cap
        + every_col_rank[:, None, :]
    )
    local_tile = segments[:, :, None] // row_count * col_tiles + segments[:, None, :] // col_count
    keep_flat = keeping.reshape(-1)
    place_flat = placing.reshape(-1)
    tile_flat = local_tile.reshape(-1)
    tile_range = lax.broadcasted_iota(jnp.int32, (1, row_tiles * col_tiles), 1)
    slot_range = lax.broadcasted_iota(jnp.int32, (1, slots_all), 1)
    tile_hot = jnp.where(keep_flat[:, None] & (tile_flat[:, None] == tile_range), 1.0, 0.0).astype(
        jnp.float32
    )
    slot_hot = jnp.where(place_flat[:, None] == slot_range, 1.0, 0.0).astype(jnp.float32)
    routing = lax.dot_general(
        tile_hot,
        slot_hot,
        (((0,), (0,)), ((), ())),
        precision=lax.Precision.HIGHEST,
        preferred_element_type=jnp.float32,
    )
    routing = routing.reshape(row_tiles, col_tiles, slots_all)
    assembled = jnp.einsum(
        "rcp,pxy->rxcy",
        routing,
        arriving,
        precision=lax.Precision.HIGHEST,
        preferred_element_type=jnp.float32,
    )
    row_scale = 1.0 / jnp.sqrt(1.0 + jnp.abs(row_diag))
    col_scale = 1.0 / jnp.sqrt(1.0 + jnp.abs(col_diag))
    scaled = assembled * row_scale[:, :, None, None] * col_scale[None, None, :, :]
    return scaled.reshape(row_tiles * TILE, col_tiles * TILE)


def solution(mesh):
    split = Mesh(mesh.devices.reshape(4, 2, 4, 4), ("row_0", "row_1", "col_0", "col_1"))
    return jax.shard_map(
        body,
        mesh=split,
        in_specs=(
            P(ROW_COL, None, None),
            P(ROW_COL, None, None),
            P(ROW_COL, None),
            P(ROW_COL),
            P(),
        ),
        out_specs=P(ROW, COL),
        check_vma=False,
    )
```

profile of v0, /device:TPU:6, one launch (start us, length us, event | category | flops | bytes accessed | tf_op | source)
XLA Modules:
  0.0 232.4 jit_solution(939685399567180532)
XLA Ops:
  0.0 0.0 copy-start
  0.0 1.0 fusion.32
  1.0 0.2 select_reduce_fusion.4
  1.2 0.2 select_reduce_fusion.3
  1.4 0.1 add.291
  1.5 0.1 add.286
  1.6 0.1 add.287
  1.6 0.1 add.279
  1.7 0.1 add.280
  1.8 0.1 add.284
  1.9 0.1 select_reduce_fusion.2
  2.0 0.1 fusion.31
  2.8 0.0 copy-done
  2.8 0.0 copy-start.3
  2.8 5.2 %fusion.2 = f32[1024,200]{0,1:T(8,128)S(1)} fusion(bf16[1,4096,1024]{2,1,0:T(8,128)(2,1)} %param.5, pred[1024]{0:T(1024)(128)(4,1)S(1)} %iota_compare_fusion.6, bf16[1,200,4096]{2,1,0:T(8,128)(2,1)S(1)} %copy-done), kind=kOutput, calls=%fused_computation.11 | convolution fusion | flops 1681915904 | bytes 10847232 | tf_op jit(solution)/shard_map/dot_general | solution.py:27
  8.0 0.0 copy-done.3
  8.0 3.8 %fusion.22 = f32[1024,1024]{1,0:T(8,128)S(1)} fusion(f32[1024,200]{0,1:T(8,128)S(1)} %fusion.2, f32[200]{0:T(256)S(1)} %bitcast.104), kind=kOutput, calls=%fused_computation.33 | convolution fusion | flops 2516787200 | bytes 5014304 | tf_op jit(solution)/shard_map/dot_general | solution.py:28
  11.9 16.0 %subtract_bitcast_fusion = f32[128,8,8,128]{3,1,2,0:T(8,128)S(1)} fusion(f32[1024,1024]{1,0:T(8,128)S(1)} %fusion.22, bf16[1,4096,1024]{2,1,0:T(8,128)(2,1)} %param.5, pred[1024]{0:T(1024)(128)(4,1)S(1)} %iota_compare_fusion.6), kind=kOutput, calls=%fused_computation.23 | convolution fusion | flops 8595177472 | bytes 16778240 | tf_op jit(solution)/shard_map/dot_general | solution.py:24
  27.9 1.0 copy.86
  29.0 2.8 %copy.61 = f32[1,8,128,8,128]{4,2,3,1,0:T(8,128)} copy(f32[1,8,128,8,128]{4,3,2,1,0:T(8,128)S(1)} %bitcast.93) | data formatting | bytes 8388608 | tf_op jit(solution)/shard_map/stack;reshape | solution.py:63
  31.7 6.5 %gather_fusion = f32[128,128,128]{2,1,0:T(8,128)} fusion(f32[1,8,128,8,128]{4,2,3,1,0:T(8,128)} %copy.61, s32[128]{0:T(128)S(1)} %get-tuple-element.27), kind=kCustom, calls=%fused_computation | custom fusion | bytes 16778752 | tf_op jit(solution)/shard_map/gather | solution.py:115
  38.2 7.2 %broadcast_select_fusion.3 = f32[128,128,128]{2,1,0:T(8,128)} fusion(f32[128,128,128]{2,1,0:T(8,128)} %gather_fusion, pred[128]{0:T(512)(128)(4,1)S(1)} %fusion.31), kind=kLoop, calls=%fused_computation.22 | loop fusion | flops 2097152 | bytes 16777344 | tf_op jit(solution)/shard_map/jit(_where)/select_n | solution.py:116
  45.5 10.9 %all-to-all-start = ((f32[128,128,128]{2,1,0:T(8,128)}), f32[128,128,128]{2,1,0:T(8,128)}, u32[]{:S(2)}, u32[]{:S(2)}) async-start(f32[128,128,128]{2,1,0:T(8,128)} %broadcast_select_fusion.3), calls=%async_computation | async-start | bytes 16777216 | tf_op jit(solution)/shard_map/all_to_all | solution.py:117
  56.4 0.0 copy-start.2
  56.4 1.1 slice_bitcast_fusion
  57.5 1.2 gather_fusion.1
  58.8 1.2 gather_fusion.2
  60.0 1.2 gather_fusion.3
  61.3 1.2 gather_fusion.4
  62.5 1.2 gather_fusion.5
  63.8 1.2 gather_fusion.6
  65.0 1.2 gather_fusion.7
  66.3 1.2 gather_fusion.8
  67.6 0.3 fusion.38
  67.9 95.1 %psum.28 = f32[96,128]{1,0:T(8,128)S(1)} all-reduce(f32[96,128]{1,0:T(8,128)S(1)} %fusion.38), channel_id=1, replica_groups=mesh['row_0'=4,'row_1'=2,'col_0'=4,'col_1'=4] {'row_0'}, use_global_device_ids=true, to_apply=%region_6.7 | all-reduce | flops 12288 | bytes 98304 | tf_op jit(solution)/shard_map/psum | solution.py:17
  163.0 3.5 %psum.29 = f32[96,128]{1,0:T(8,128)S(1)} all-reduce(f32[96,128]{1,0:T(8,128)S(1)} %psum.28), channel_id=1, replica_groups=mesh['row_0'=4,'row_1'=2,'col_0'=4,'col_1'=4] {'row_1'}, use_global_device_ids=true, to_apply=%region_7.8 | all-reduce | flops 12288 | bytes 98304 | tf_op jit(solution)/shard_map/psum | solution.py:17
  166.5 19.1 %psum.30 = f32[96,128]{1,0:T(8,128)S(1)} all-reduce(f32[96,128]{1,0:T(8,128)S(1)} %psum.29), channel_id=1, replica_groups=mesh['row_0'=4,'row_1'=2,'col_0'=4,'col_1'=4] {'col_0'}, use_global_device_ids=true, to_apply=%region_8.9 | all-reduce | flops 12288 | bytes 98304 | tf_op jit(solution)/shard_map/psum | solution.py:17
  185.6 20.7 %psum.31 = f32[96,128]{1,0:T(8,128)S(1)} all-reduce(f32[96,128]{1,0:T(8,128)S(1)} %psum.30), channel_id=1, replica_groups=mesh['row_0'=4,'row_1'=2,'col_0'=4,'col_1'=4] {'col_1'}, use_global_device_ids=true, to_apply=%region_9.10 | all-reduce | flops 12288 | bytes 98304 | tf_op jit(solution)/shard_map/psum | solution.py:17
  206.3 0.1 copy.84
  206.4 0.0 copy-done.2
  206.4 0.1 select_reduce_fusion.1
  206.5 0.1 copy.67
  206.6 0.1 copy.66
  206.7 0.2 add_add_fusion
  206.9 0.3 add.308
  207.2 0.1 copy.65
  207.3 0.1 copy.64
  207.4 0.2 broadcast_add_fusion
  207.6 0.3 add.303
  207.8 0.1 copy.63
  208.0 0.1 copy.62
  208.1 0.2 broadcast_and_fusion
  208.3 0.3 and.194
  208.6 3.9 %fusion.7 = f32[72,128]{1,0:T(8,128)S(1)} fusion(s32[8192]{0:T(1024)S(1)} %add.308, s32[8192]{0:T(1024)S(1)} %add.303, pred[8192]{0:T(1024)(128)(4,1)S(1)} %and.194), kind=kOutput, calls=%fused_computation.19 | convolution fusion | flops 909836288 | bytes 110592 | tf_op jit(solution)/shard_map/dot_general | solution.py:141
  212.5 0.0 all-to-all-done
  212.5 15.0 %fusion.6 = f32[12,128,6,128]{3,0,2,1:T(8,128)S(1)} fusion(f32[6,128]{1,0:T(8,128)S(1)} %fusion.37, f32[12,128]{0,1:T(8,128)S(1)} %rsqrt_bitcast_fusion, f32[128,128,128,1]{2,1,0,3:T(8,128)} %bitcast.6, f32[12,6,128]{2,1,0:T(8,128)S(1)} %reshape.560), kind=kOutput, calls=%fused_computation.17 | convolution fusion | flops 1814298624 | bytes 13153280 | tf_op jit(solution)/shard_map/rcp,pxy->rxcy/dot_general | solution.py:149
  227.5 0.0 copy-start.1
  227.5 1.5 copy.80
  229.1 3.3 %copy.104 = f32[192,8,6,128]{3,1,2,0:T(8,128)} copy(f32[192,8,6,128]{3,2,1,0:T(8,128)S(1)} %bitcast.92) | data formatting | bytes 9437184
  232.4 0.0 copy-done.1
  (15 shorter events, 0.2 us)
Async XLA Ops:
  0.0 2.8 %copy-start = (bf16[1,200,4096]{2,1,0:T(8,128)(2,1)S(1)}, bf16[1,200,4096]{2,1,0:T(8,128)(2,1)}, u32[]{:S(2)}) copy-start(bf16[1,200,4096]{2,1,0:T(8,128)(2,1)} %param.6) | copy-start | bytes 4915204
  2.8 5.3 %copy-start.3 = (f32[1,200]{1,0:T(1,128)S(1)}, f32[1,200]{1,0:T(1,128)}, u32[]{:S(2)}) copy-start(f32[1,200]{1,0:T(1,128)} %param.7) | copy-start | bytes 2404
  45.5 167.1 %all-to-all-start = ((f32[128,128,128]{2,1,0:T(8,128)}), f32[128,128,128]{2,1,0:T(8,128)}, u32[]{:S(2)}, u32[]{:S(2)}) async-start(f32[128,128,128]{2,1,0:T(8,128)} %broadcast_select_fusion.3), calls=%async_computation | async-start | bytes 16777216 | tf_op jit(solution)/shard_map/all_to_all | solution.py:117
  56.4 150.0 %copy-start.2 = (s32[128,8]{0,1:T(8,128)S(1)}, s32[128,8]{0,1:T(8,128)}, u32[]{:S(2)}) copy-start(s32[128,8]{0,1:T(8,128)} %param.9) | copy-start | bytes 12292
  227.5 4.9 %copy-start.1 = (bf16[1,200,4096]{2,1,0:T(8,128)(2,1)S(1)}, bf16[1,200,4096]{2,1,0:T(8,128)(2,1)}, u32[]{:S(2)}) copy-start(bf16[1,200,4096]{2,1,0:T(8,128)(2,1)} %param.6) | copy-start | bytes 4915204
where the time goes:
time: 236 us; the launch traced here: 232 us
  blocking collectives  138 us (58%)
  matrix products  44.3 us (19%)
  local copies, waits for them, and re-layouts  28.3 us (12%)
  starting transfers between devices  10.9 us (5%)
  other arithmetic  9.59 us (4%)
    psum x4, blocking collectives, by_axis(): return functools.reduce(lax.psum, axes, shard)  138 us
    dot_general x1, matrix products, substructure_block(): lax.dot_general(masked, masked, (((0,), (0,)), ((), ())), preferred_eleme...  16 us
    dot_general x1, matrix products, body(): jnp.einsum('rcp,pxy->rxcy', routing, arriving, precision=lax.Precision.HI...  15 us
    all_to_all x1, starting transfers between devices, body(): lax.all_to_all(outgoing, ROW_COL, split_axis=0, concat_axis=0, tiled=True)  10.9 us
    gather x8, local copies, waits for them, and re-layouts, body(): jnp.diagonal(blocks[:, index, :, index, :], axis1=1, axis2=2)  9.96 us
    select_n x1, other arithmetic, body(): jnp.where(filled[:, None, None], outgoing, jnp.zeros((), jnp.float32))  7.22 us
    gather x1, local copies, waits for them, and re-layouts, body(): outgoing = blocks[member_src, row_src, :, col_src, :]  6.49 us
    dot_general x1, matrix products, substructure_block(): projected = jnp.dot(modal_rows, masked, preferred_element_type=jnp.float32)  5.24 us
  transfers between devices with their start and end apart: 1, of which 0 were waited for; matrix products, arithmetic and copies ran while one was open for 8% of the time, Pallas kernels for 0%

commit v1 on v0

v1 whole, which is shorter than its diff:
```python
import functools

import jax
import jax.numpy as jnp
from jax import lax
from jax.experimental import pallas as pl
from jax.experimental.pallas import tpu as pltpu
from jax.sharding import PartitionSpec as P

TILE = 128
CHUNKS = 4
PART = TILE // CHUNKS
CLASSES = 8
PLANE = 32
RING = 4
ROW_TILES = 12
COL_TILES = 6
DEPTH = 1024
F32 = jnp.float32
BF16 = jnp.bfloat16
MESH = pl.DeviceIdType.MESH
HIGH = lax.Precision.HIGHEST


def over_rows(left, right):
    return lax.dot_general(left, right, (((0,), (0,)), ((), ())), preferred_element_type=F32)


def block_kernel(steps, perm, width, *refs):
    columns, (modes, weights, out, diag, masked, acc, proj) = refs[:CLASSES], refs[CLASSES:]
    step = pl.program_id(0)
    for k in range(CLASSES):
        lane = lax.broadcasted_iota(jnp.int32, (DEPTH, TILE), 1) + perm[k] * TILE
        masked[:, k * TILE : (k + 1) * TILE] = jnp.where(
            lane < width[0], columns[k][0], jnp.zeros((), BF16)
        )

    @pl.when(step == 0)
    def _():
        acc[...] = jnp.zeros_like(acc)
        proj[...] = jnp.zeros_like(proj)

    proj[...] += jnp.dot(modes[0], masked[...], preferred_element_type=F32)
    for m in range(0, 1024, 256):
        acc[m : m + 256, m:] += over_rows(masked[:, m : m + 256], masked[:, m:])

    @pl.when(step == steps - 1)
    def _():
        p = proj[...]
        w = p * weights[...]
        p_hi, w_hi = p.astype(BF16), w.astype(BF16)
        p_lo = (p - p_hi.astype(F32)).astype(BF16)
        w_lo = (w - w_hi.astype(F32)).astype(BF16)
        left = jnp.concatenate([w_hi, w_hi, w_lo], 0)
        right = jnp.concatenate([p_hi, p_lo, p_hi], 0)
        for m in range(0, 1024, 256):
            acc[m : m + 256, m:] -= over_rows(left[:, m : m + 256], right[:, m:])
        for m in range(256, 1024, 256):
            for n in range(0, m, 256):
                acc[m : m + 256, n : n + 256] = acc[n : n + 256, m : m + 256].T
        same = lax.broadcasted_iota(jnp.int32, (TILE, TILE), 0) == lax.broadcasted_iota(
            jnp.int32, (TILE, TILE), 1
        )
        for k in range(CLASSES):
            for m in range(CLASSES):
                for q in range(CHUNKS):
                    rows = k * TILE + q * PART
                    out[q, k, m % 4, m // 4] = acc[rows : rows + PART, m * TILE : (m + 1) * TILE]
            tile = acc[k * TILE : (k + 1) * TILE, k * TILE : (k + 1) * TILE]
            diag[k : k + 1, :] = jnp.sum(jnp.where(same, tile, 0.0), axis=0, keepdims=True)


def make_block(coupling, modes, flexibility, width, perm):
    steps = coupling.shape[1] // DEPTH
    count = modes.shape[1]

    def column(k, i, perm, width):
        return (0, i, perm[k])

    return pl.pallas_call(
        functools.partial(block_kernel, steps),
        grid_spec=pltpu.PrefetchScalarGridSpec(
            num_scalar_prefetch=2,
            grid=(steps,),
            in_specs=[
                pl.BlockSpec((1, DEPTH, TILE), functools.partial(column, k)) for k in range(CLASSES)
            ]
            + [
                pl.BlockSpec((1, count, DEPTH), lambda i, perm, width: (0, 0, i)),
                pl.BlockSpec((count, 1), lambda i, perm, width: (0, 0)),
            ],
            out_specs=[
                pl.BlockSpec((CHUNKS, 8, 4, 2, PART, TILE), lambda i, perm, width: (0,) * 6),
                pl.BlockSpec((CLASSES, TILE), lambda i, perm, width: (0, 0)),
            ],
            scratch_shapes=[
                pltpu.VMEM((DEPTH, 1024), BF16),
                pltpu.VMEM((1024, 1024), F32),
                pltpu.VMEM((count, 1024), F32),
            ],
        ),
        out_shape=[
            jax.ShapeDtypeStruct((CHUNKS, 8, 4, 2, PART, TILE), F32),
            jax.ShapeDtypeStruct((CLASSES, TILE), F32),
        ],
        compiler_params=pltpu.CompilerParams(vmem_limit_bytes=48 << 20),
        name="block",
    )(perm, width, *([coupling] * CLASSES), modes, flexibility.reshape(count, 1))


def exchange_kernel(cap, order, tiles, diag, ring_out, own_out, diag_out, *scratch):
    held, scratch = scratch[:CHUNKS], scratch[CHUNKS:]
    send, diag_held, diag_send, a_send, a_recv, b_send, b_recv, o_sem, d_sem = scratch
    row, col = lax.axis_index("row"), lax.axis_index("col")
    y, z = col // 4, col % 4
    mine = row * 4 + z

    def plane_peer(step):
        there = lax.rem(mine + step, PLANE)
        return there, (there // 4, y * 4 + lax.rem(there, 4))

    def ring_peer(step):
        return (row, lax.rem(y + step, RING) * 4 + z)

    barrier = pltpu.get_barrier_semaphore()

    def greet(step, carry):
        pl.semaphore_signal(barrier, inc=1, device_id=plane_peer(step)[1], device_id_type=MESH)
        return carry

    lax.fori_loop(1, PLANE, greet, 0)
    for step in range(1, RING):
        pl.semaphore_signal(barrier, inc=1, device_id=ring_peer(step), device_id_type=MESH)
    pl.semaphore_wait(barrier, PLANE - 1 + RING - 1)

    own_copies = []

    def local(src, dst, sem):
        copy = pltpu.make_async_copy(src, dst, sem)
        copy.start()
        return copy

    def send_diag(step, carry):
        pltpu.make_async_remote_copy(
            src_ref=diag,
            dst_ref=diag_held.at[mine],
            send_sem=d_sem.at[0],
            recv_sem=d_sem.at[1],
            device_id=plane_peer(step)[1],
            device_id_type=MESH,
        ).start()
        return carry

    lax.fori_loop(1, PLANE, send_diag, 0)
    own_diag = local(diag, diag_held.at[mine], d_sem.at[2])
    for q in range(CHUNKS):

        def send_tiles(step, carry, q=q):
            there, peer = plane_peer(step)
            pltpu.make_async_remote_copy(
                src_ref=tiles.at[q, there // 4, lax.rem(there, 4)],
                dst_ref=held[q].at[mine],
                send_sem=a_send.at[q],
                recv_sem=a_recv.at[q],
                device_id=peer,
                device_id_type=MESH,
            ).start()
            return carry

        lax.fori_loop(1, PLANE, send_tiles, 0)
        own_copies.append(local(tiles.at[q, row, z], held[q].at[mine], o_sem.at[0, q]))

    def whole(ref, sem):
        part = ref.at[pl.ds(0, PLANE - 1)]
        pltpu.make_async_copy(part, part, sem).wait()

    pending = []
    whole(diag_held, d_sem.at[1])
    own_diag.wait()

    def pick(i, carry):
        for parity in range(2):
            diag_send[parity, 0, pl.ds(i, 1), :] = diag_held[i, pl.ds(row, 1), :]
            diag_send[parity, 1, pl.ds(i, 1), :] = diag_held[i, pl.ds(4 * parity + z, 1), :]
        return carry

    lax.fori_loop(0, PLANE, pick, 0)
    here = local(diag_send.at[lax.rem(y, 2)], diag_out.at[0], d_sem.at[3])
    for step in range(1, RING):
        copy = pltpu.make_async_remote_copy(
            src_ref=diag_send.at[lax.rem(y + step, 2)],
            dst_ref=diag_out.at[step],
            send_sem=b_send.at[CHUNKS, step - 1],
            recv_sem=b_recv.at[CHUNKS, step - 1],
            device_id=ring_peer(step),
            device_id_type=MESH,
        )
        copy.start()
        pending.append(copy)
    for q in range(CHUNKS):
        whole(held[q], a_recv.at[q])
        own_copies[q].wait()
        for step in range(1, RING):
            parity = lax.rem(y + step, 2)

            def arrange(j, carry, q=q, step=step, parity=parity):
                send[q, step - 1, j] = held[q][order[step - 1, j], parity]
                return carry

            lax.fori_loop(0, cap, arrange, 0)
            copy = pltpu.make_async_remote_copy(
                src_ref=send.at[q, step - 1],
                dst_ref=ring_out.at[q, step - 1, pl.ds(0, cap)],
                send_sem=b_send.at[q, step - 1],
                recv_sem=b_recv.at[q, step - 1],
                device_id=ring_peer(step),
                device_id_type=MESH,
            )
            copy.start()
            pending.append(copy)
        own_copies[q] = local(held[q].at[:, lax.rem(y, 2)], own_out.at[q], o_sem.at[1, q])
    for copy in pending:
        copy.wait()
    for copy in own_copies:
        copy.wait()
    here.wait()
    whole(diag_held, d_sem.at[0])
    for q in range(CHUNKS):
        whole(held[q], a_send.at[q])


def exchange(cap, order, tiles, diag):
    dma = pltpu.SemaphoreType.DMA
    anywhere = pl.BlockSpec(memory_space=pl.ANY)
    return pl.pallas_call(
        functools.partial(exchange_kernel, cap),
        in_specs=[pl.BlockSpec(memory_space=pltpu.SMEM), anywhere, anywhere],
        out_specs=[anywhere] * 3,
        out_shape=[
            jax.ShapeDtypeStruct((CHUNKS, RING - 1, PLANE, PART, TILE), F32),
            jax.ShapeDtypeStruct((CHUNKS, PLANE, PART, TILE), F32),
            jax.ShapeDtypeStruct((RING, 2, PLANE, TILE), F32),
        ],
        scratch_shapes=[pltpu.VMEM((PLANE, 2, PART, TILE), F32)] * CHUNKS
        + [
            pltpu.VMEM((CHUNKS, RING - 1, cap, PART, TILE), F32),
            pltpu.VMEM((PLANE, CLASSES, TILE), F32),
            pltpu.VMEM((2, 2, PLANE, TILE), F32),
            dma((CHUNKS,)),
            dma((CHUNKS,)),
            dma((CHUNKS + 1, RING - 1)),
            dma((CHUNKS + 1, RING - 1)),
            dma((2, CHUNKS)),
            dma((4,)),
        ],
        compiler_params=pltpu.CompilerParams(
            collective_id=cap, has_side_effects=True, vmem_limit_bytes=40 << 20
        ),
        name="exchange",
    )(order, tiles, diag)


def assemble_kernel(count, place, ring, own, diag, row_hot, col_hot, out, row_scale, col_scale):
    chunk = pl.program_id(0)

    @pl.when(chunk == 0)
    def _():
        rows = lax.dot_general(
            diag[:, 0].reshape(RING * PLANE, TILE),
            row_hot[...],
            (((0,), (0,)), ((), ())),
            precision=HIGH,
            preferred_element_type=F32,
        )
        cols = jnp.dot(
            col_hot[...],
            diag[:, 1].reshape(RING * PLANE, TILE),
            precision=HIGH,
            preferred_element_type=F32,
        )
        row_scale[...] = 1.0 / jnp.sqrt(1.0 + jnp.abs(rows))
        col_scale[...] = 1.0 / jnp.sqrt(1.0 + jnp.abs(cols))

    out[...] = jnp.zeros_like(out)
    for d in range(RING):

        def add(j, carry, d=d):
            code = place[d, j]
            tile = own[0, code & 31] if d == 0 else ring[0, d - 1, j]
            across = pl.ds(pl.multiple_of((code >> 9) * TILE, TILE), TILE)
            out[(code >> 5) & 15, 0, :, across] += tile
            return carry

        lax.fori_loop(0, count[d], add, 0)
    inside = pl.ds(pl.multiple_of(chunk * PART, PART), PART)
    for g in range(ROW_TILES):
        for h in range(COL_TILES):
            scale = row_scale[inside, g : g + 1] * col_scale[h : h + 1, :]
            out[g, 0, :, h * TILE : (h + 1) * TILE] *= scale


def assemble(cap, count, place, ring, own, diag, row_hot, col_hot):
    return pl.pallas_call(
        assemble_kernel,
        grid_spec=pltpu.PrefetchScalarGridSpec(
            num_scalar_prefetch=2,
            grid=(CHUNKS,),
            in_specs=[
                pl.BlockSpec((1, RING - 1, cap, PART, TILE), lambda q, n, p: (q, 0, 0, 0, 0)),
                pl.BlockSpec((1, PLANE, PART, TILE), lambda q, n, p: (q, 0, 0, 0)),
                pl.BlockSpec((RING, 2, PLANE, TILE), lambda q, n, p: (0, 0, 0, 0)),
                pl.BlockSpec((RING * PLANE, 16), lambda q, n, p: (0, 0)),
                pl.BlockSpec((8, RING * PLANE), lambda q, n, p: (0, 0)),
            ],
            out_specs=pl.BlockSpec(
                (ROW_TILES, 1, PART, COL_TILES * TILE), lambda q, n, p: (0, q, 0, 0)
            ),
            scratch_shapes=[pltpu.VMEM((TILE, 16), F32), pltpu.VMEM((8, TILE), F32)],
        ),
        out_shape=jax.ShapeDtypeStruct((ROW_TILES, CHUNKS, PART, COL_TILES * TILE), F32),
        compiler_params=pltpu.CompilerParams(vmem_limit_bytes=40 << 20),
        name="assemble",
    )(count, place, ring, own, diag, row_hot, col_hot)


def sum_where(mask, values, axis):
    return jnp.sum(jnp.where(mask, values, 0), axis=axis)


def places(segments, row, col):
    y, z = col // 4, col % 4
    iota8 = jnp.arange(8, dtype=jnp.int32)
    slots = jnp.arange(PLANE, dtype=jnp.int32)
    steps = jnp.arange(RING, dtype=jnp.int32)
    in_class = (segments & 7)[:, :, None] == iota8
    by_class = sum_where(in_class, segments[:, :, None], 1)
    mine = jnp.arange(128, dtype=jnp.int32)[:, None] == row * 16 + col
    perm = sum_where(in_class & mine[:, :, None], iota8[None, :, None], (0, 1))
    planes = by_class.reshape(8, RING, 4, 8)
    ring = (y - steps) & 3
    from_plane = ring[:, None, None, None, None] == steps[None, None, :, None, None]
    held = sum_where(from_plane, planes[None], 2).reshape(RING, PLANE, 8)
    row_seg = sum_where(iota8 == row, held, 2)
    col_seg = sum_where(iota8 == (col & 7), held, 2)
    goes = (y + steps) & 3
    out_seg = sum_where(iota8 == (4 * (goes & 1) + z)[:, None, None], held[:1], 2)
    arrives = ((col_seg >> 3) & 1) == (col >> 3)
    leaves = ((out_seg >> 3) & 1) == (goes >> 1)[:, None]
    flags = jnp.stack([arrives, leaves])
    before = slots[:, None] > slots[None, :]
    rank = jnp.sum((flags[:, :, None, :] & before).astype(jnp.int32), axis=3)
    lands = flags[:, :, None, :] & (rank[:, :, None, :] == slots[:, None])
    codes = slots + 32 * (row_seg >> 3) + 512 * (col_seg >> 4)
    values = jnp.stack([codes, jnp.broadcast_to(slots, codes.shape)])
    table = sum_where(lands, values[:, :, None, :], 3)
    count = jnp.sum(arrives.astype(jnp.int32), axis=1)
    row_hot = (row_seg.reshape(-1)[:, None] >> 3) == jnp.arange(16, dtype=jnp.int32)
    col_place = jnp.where(arrives, col_seg >> 4, -1).reshape(-1)
    col_hot = col_place[None, :] == iota8[:, None]
    return perm, table[1, 1:], count, table[0], row_hot.astype(F32), col_hot.astype(F32)


def body(coupling, modes, flexibility, widths, segments):
    row, col = lax.axis_index("row"), lax.axis_index("col")
    perm, order, count, place, row_hot, col_hot = places(segments, row, col)
    tiles, diag = make_block(coupling, modes, flexibility[0], widths, perm)
    ring, own, diags = exchange(PLANE, order, tiles, diag)
    out = assemble(PLANE, count, place, ring, own, diags, row_hot, col_hot)
    return out.reshape(ROW_TILES * TILE, COL_TILES * TILE)


def solution(mesh):
    both = ("row", "col")
    return jax.shard_map(
        body,
        mesh=mesh,
        in_specs=(P(both, None, None), P(both, None, None), P(both, None), P(both), P()),
        out_specs=P("row", "col"),
        check_vma=False,
    )
```

time: 236 us -> 154 us (0.65)
  the two profiles are of different devices: /device:TPU:6 before, /device:TPU:2 now
where the time goes in v1:
time: 154 us; the launch traced here: 153 us
  Pallas kernels  146 us (95%)
  local copies, waits for them, and re-layouts  3.41 us (2%)
  other arithmetic  3.32 us (2%)
    pallas_call x1, Pallas kernels, exchange(): pl.pallas_call(functools.partial(exchange_kernel, cap), in_specs=[pl.Bloc...  124 us
    pallas_call x1, Pallas kernels, make_block(): pl.pallas_call(functools.partial(block_kernel, steps), grid_spec=pltpu.Pr...  14.7 us
    pallas_call x1, Pallas kernels, assemble(): pl.pallas_call(assemble_kernel, grid_spec=pltpu.PrefetchScalarGridSpec(nu...  7.1 us

profile of v1, /device:TPU:2, one launch (start us, length us, event | category | flops | bytes accessed | tf_op | source)
XLA Modules:
  0.0 153.4 jit_solution(12982998440165542316)
XLA Ops:
  0.7 0.1 iota_compare_fusion.5
  0.8 0.1 iota_compare_fusion.6
  0.9 0.7 broadcast_and_fusion
  1.5 0.8 select_reduce_fusion.4
  2.4 0.1 copy.18
  2.5 0.1 select_reduce_fusion
  2.6 0.6 select_reduce_fusion.2
  3.3 0.1 copy.22
  3.3 0.1 select_reduce_fusion.6
  3.4 0.1 bitcast_compare_fusion
  3.5 0.1 copy.26
  3.6 0.1 shift_right_arithmetic.82
  3.7 0.1 copy.23
  3.8 0.1 mul.45
  3.9 0.2 convert_reduce_fusion.1.count
  4.1 0.1 copy.20
  4.2 0.1 eq.161
  4.3 0.2 convert_reduce_fusion
  4.5 0.1 copy.27
  4.6 0.1 select_n.61
  4.7 0.1 copy.24
  4.8 0.1 mul.48
  4.9 0.2 select_reduce_fusion.1
  5.2 0.1 fusion.1.row_hot
  5.3 0.8 copy.25.refs_9_
  6.1 0.0 copy-start
  6.1 1.4 copy-done
  7.5 14.7 %block.1 = (f32[4,8,4,2,32,128]{5,4,3,2,1,0:T(8,128)S(1)}, f32[8,128]{1,0:T(8,128)S(1)}) custom-call(s32[8]{0:T(128)S(1)} %get-tuple-element.17.perm, s32[1]{0:T(128)S(6)} %copy.28.width, bf16[1,4096,1024]{2,1,0:T(8,128)(2,1)} %refs_7_.1, bf16[1,4096,1024]{2,1,0:T(8,128)(2,1)} %refs_7_.1, bf16[1,4096,1024]{2,1,0:T(8,128)(2,1)} %refs_7_.1, ...), custom_call_target="tpu_custom_call" | custom-call | tf_op jit(solution)/shard_map/block/pallas_call | solution.py:80
  22.2 124.1 %exchange.1 = (f32[4,3,32,32,128]{4,3,2,1,0:T(8,128)S(1)}, f32[4,32,32,128]{3,2,1,0:T(8,128)S(1)}, f32[4,2,32,128]{3,2,1,0:T(8,128)S(1)}) custom-call(s32[3,32]{1,0:T(4,128)S(1)} %slice_bitcast_fusion.order, f32[4,8,4,2,32,128]{5,4,3,2,1,0:T(8,128)S(1)} %get-tuple-element.10.tiles, f32[8,128]{1,0:T(8,128)S(1)} %get-tuple-element.11.diag), custom_call_target="tpu_custom_call" | custom-call | tf_op jit(solution)/shard_map/exchange/pallas_call | solution.py:235
  146.4 7.1 %assemble.1 = f32[12,4,32,768]{3,2,1,0:T(8,128)} custom-call(s32[4]{0:T(128)S(1)} %convert_reduce_fusion.1.count, s32[4,32]{1,0:T(4,128)S(1)} %slice_bitcast_fusion.1.place, f32[4,3,32,32,128]{4,3,2,1,0:T(8,128)S(1)} %get-tuple-element.12.ring, f32[4,32,32,128]{3,2,1,0:T(8,128)S(1)} %get-tuple-element.13.own, f32[4,2,32,128]{3,2,1,0:T(8,128)S(1)} %get-tuple-element.14.diag, ...), custom_call_target="tpu_custom_call" | custom-call | tf_op jit(solution)/shard_map/assemble/pallas_call | solution.py:303
  (17 shorter events, 0.1 us)
Async XLA Ops:
  6.1 1.4 copy-start

commit v2 on v1

--- a/solution.py
+++ b/solution.py
@@ -8,7 +8,7 @@
 from jax.sharding import PartitionSpec as P
 
 TILE = 128
-CHUNKS = 4
+CHUNKS = 8
 PART = TILE // CHUNKS
 CLASSES = 8
 PLANE = 32
@@ -16,6 +16,7 @@
 ROW_TILES = 12
 COL_TILES = 6
 DEPTH = 1024
+CAPS = (20, 22, 24, PLANE)
 F32 = jnp.float32
 BF16 = jnp.bfloat16
 MESH = pl.DeviceIdType.MESH
@@ -357,15 +358,29 @@
     row_hot = (row_seg.reshape(-1)[:, None] >> 3) == jnp.arange(16, dtype=jnp.int32)
     col_place = jnp.where(arrives, col_seg >> 4, -1).reshape(-1)
     col_hot = col_place[None, :] == iota8[:, None]
-    return perm, table[1, 1:], count, table[0], row_hot.astype(F32), col_hot.astype(F32)
+    high = jnp.sum((planes >> 3) & 1, axis=(0, 2))
+    held_by = jnp.stack([PLANE - high, high])
+    goal = 2 * steps[:2, None, None] + (iota8 >> 2)
+    need = jnp.max(jnp.where(goal == steps[:, None], 0, held_by))
+    return perm, table[1, 1:], need, count, table[0], row_hot.astype(F32), col_hot.astype(F32)
 
 
 def body(coupling, modes, flexibility, widths, segments):
     row, col = lax.axis_index("row"), lax.axis_index("col")
-    perm, order, count, place, row_hot, col_hot = places(segments, row, col)
+    perm, order, need, count, place, row_hot, col_hot = places(segments, row, col)
     tiles, diag = make_block(coupling, modes, flexibility[0], widths, perm)
-    ring, own, diags = exchange(PLANE, order, tiles, diag)
-    out = assemble(PLANE, count, place, ring, own, diags, row_hot, col_hot)
+
+    def within(cap):
+        def run(order, tiles, diag, count, place, row_hot, col_hot):
+            ring, own, diags = exchange(cap, order, tiles, diag)
+            return assemble(cap, count, place, ring, own, diags, row_hot, col_hot)
+
+        return run
+
+    level = jnp.sum((need > jnp.array(CAPS[:-1])).astype(jnp.int32))
+    out = lax.switch(
+        level, [within(cap) for cap in CAPS], order, tiles, diag, count, place, row_hot, col_hot
+    )
     return out.reshape(ROW_TILES * TILE, COL_TILES * TILE)
 
 

time: 154 us -> 125 us (0.81)
  the two profiles are of different devices: /device:TPU:2 before, /device:TPU:6 now
where the time goes in v2:
time: 125 us
  Pallas kernels  112 us (90%)
  other arithmetic  6.11 us (5%)
  local copies, waits for them, and re-layouts  5.62 us (4%)
  between operations  1.52 us (1%)
    pallas_call x1, Pallas kernels, exchange(): pl.pallas_call(functools.partial(exchange_kernel, cap), in_specs=[pl.Bloc...  85.1 us
    pallas_call x1, Pallas kernels, make_block(): pl.pallas_call(functools.partial(block_kernel, steps), grid_spec=pltpu.Pr...  16.7 us
    pallas_call x1, Pallas kernels, assemble(): pl.pallas_call(assemble_kernel, grid_spec=pltpu.PrefetchScalarGridSpec(nu...  9.89 us
    unnamed x4, local copies, waits for them, and re-layouts  3.61 us

profile of v2, /device:TPU:6, one launch (start us, length us, event | category | flops | bytes accessed | tf_op | source)
XLA Modules:
  0.0 125.0 jit_solution(14184040361087599354)
XLA Ops:
  0.7 0.1 iota_compare_fusion.5
  0.8 0.1 iota_compare_fusion.6
  0.9 0.1 broadcast_add_fusion
  0.9 0.7 broadcast_and_fusion
  1.6 0.8 select_reduce_fusion.7
  2.5 0.1 copy.38
  2.6 0.1 select_reduce_fusion.4
  2.7 0.6 fusion.2
  3.4 2.0 %fusion.4 = s32[]{:T(128)} fusion(s32[3]{0:T(128)} %constant.67.clone, s32[]{:T(128)} %fusion.2), kind=kLoop, calls=%fused_computation.48 | loop fusion | flops 8 | bytes 20 | tf_op jit(solution)/shard_map/reduce_sum | solution.py:380
  6.1 0.6 select_reduce_fusion.5
  6.7 0.1 copy.43
  6.8 0.1 select_reduce_fusion.9
  6.9 0.1 bitcast_compare_fusion
  7.0 0.1 copy.47
  7.1 0.1 mul.50
  7.2 0.1 copy.45
  7.3 0.1 shift_right_arithmetic.98
  7.4 0.1 copy.41
  7.5 0.1 eq.177
  7.6 0.1 copy.46
  7.7 0.1 select_n.66
  7.8 0.1 copy.48
  7.9 0.1 mul.53
  8.1 0.1 fusion
  8.2 0.8 copy.44.refs_9_
  9.0 0.0 copy-start
  9.0 1.4 %copy-done = bf16[1,200,4096]{2,1,0:T(8,128)(2,1)S(1)} copy-done((bf16[1,200,4096]{2,1,0:T(8,128)(2,1)S(1)}, bf16[1,200,4096]{2,1,0:T(8,128)(2,1)}, u32[]{:S(2)}) %copy-start) | copy-done | bytes 1638424
  10.4 16.7 %block.1 = (f32[8,8,4,2,16,128]{5,4,3,2,1,0:T(8,128)}, f32[8,128]{1,0:T(8,128)S(1)}) custom-call(s32[8]{0:T(128)S(1)} %get-tuple-element.290.perm, s32[1]{0:T(128)S(6)} %copy.54.width, bf16[1,4096,1024]{2,1,0:T(8,128)(2,1)} %refs_7_.1, bf16[1,4096,1024]{2,1,0:T(8,128)(2,1)} %refs_7_.1, bf16[1,4096,1024]{2,1,0:T(8,128)(2,1)} %refs_7_.1, ...), custom_call_target="tpu_custom_call" | custom-call | tf_op jit(solution)/shard_map/block/pallas_call | solution.py:81
  27.1 95.7 %conditional.1 = (f32[1536,768]{1,0:T(8,128)S(1)}) conditional(s32[]{:T(128)} %clamp.3, (s32[4,8,4]{1,2,0:T(4,128)S(1)}, pred[2,4,32,32]{3,2,1,0:T(8,128)(4,1)S(1)}, f32[8,8,4,2,16,128]{5,4,3,2,1,0:T(8,128)}, f32[8,128]{1,0:T(8,128)S(1)}, f32[128,16]{1,0:T(8,128)S(1)}, /*index=5*/f32[8,128]{1,0:T(8,128)S(1)}, ...), branch_computations={%region_11.13_spmd.clone, %region_13.15_spmd.clone, %region_15.17_... | conditional | flops 40572 | bytes 80168 | solution.py:381
  27.1 0.2 reduce_sum.142.count
  27.3 0.2 reduce_sum.144
  27.5 0.2 select_reduce_fusion.1
  27.7 85.1 %exchange.5 = (f32[8,3,32,16,128]{4,3,2,1,0:T(8,128)S(1)}, f32[8,32,16,128]{3,2,1,0:T(8,128)S(1)}, f32[4,2,32,128]{3,2,1,0:T(8,128)S(1)}) custom-call(s32[3,32]{1,0:T(4,128)S(1)} %slice_bitcast_fusion.2.order, f32[8,8,4,2,16,128]{5,4,3,2,1,0:T(8,128)} %get-tuple-element.211.tiles, f32[8,128]{1,0:T(8,128)S(1)} %get-tuple-element.212.diag), custom_call_target="tpu_custom_call" | custom-call | tf_op jit(solution)/shard_map/cond/branch_1_fun/exchange/pallas_call | solution.py:236
  112.9 9.9 %assemble.5 = f32[12,8,16,768]{3,2,1,0:T(8,128)S(1)} custom-call(s32[4]{0:T(128)S(1)} %reduce_sum.142.count, s32[4,32]{1,0:T(4,128)S(1)} %slice_bitcast_fusion.3.place, f32[8,3,32,16,128]{4,3,2,1,0:T(8,128)S(1)} %get-tuple-element.213.ring, f32[8,32,16,128]{3,2,1,0:T(8,128)S(1)} %get-tuple-element.214.own, f32[4,2,32,128]{3,2,1,0:T(8,128)S(1)} %get-tuple-element.215.diag, ...), custom_call_target="tpu_custom_call" | custom-call | tf_op jit(solution)/shard_map/cond/branch_1_fun/assemble/pallas_call | solution.py:304
  122.8 0.0 copy-start.1
  122.8 2.2 %copy-done.1 = f32[1536,768]{1,0:T(8,128)} copy-done((f32[1536,768]{1,0:T(8,128)}, f32[1536,768]{1,0:T(8,128)S(1)}, u32[]{:S(2)}) %copy-start.1) | copy-done | bytes 4718616
  (26 shorter events, 0.2 us)
Async XLA Ops:
  9.0 1.4 %copy-start = (bf16[1,200,4096]{2,1,0:T(8,128)(2,1)S(1)}, bf16[1,200,4096]{2,1,0:T(8,128)(2,1)}, u32[]{:S(2)}) copy-start(bf16[1,200,4096]{2,1,0:T(8,128)(2,1)} %refs_8_.1) | copy-start | bytes 4915204
  122.8 2.2 %copy-start.1 = (f32[1536,768]{1,0:T(8,128)}, f32[1536,768]{1,0:T(8,128)S(1)}, u32[]{:S(2)}) copy-start(f32[1536,768]{1,0:T(8,128)S(1)} %get-tuple-element.305) | copy-start | bytes 14155780

commit v3 on v2

--- a/solution.py
+++ b/solution.py
@@ -16,7 +16,8 @@
 ROW_TILES = 12
 COL_TILES = 6
 DEPTH = 1024
-CAPS = (20, 22, 24, PLANE)
+GROUP = 4
+CAPS = (20, 22, 23, 24, 26, PLANE)
 F32 = jnp.float32
 BF16 = jnp.bfloat16
 MESH = pl.DeviceIdType.MESH
@@ -48,7 +49,11 @@
     @pl.when(step == steps - 1)
     def _():
         p = proj[...]
-        w = p * weights[...]
+        count = p.shape[0]
+        square = lax.broadcasted_iota(jnp.int32, (count, count), 0) == lax.broadcasted_iota(
+            jnp.int32, (count, count), 1
+        )
+        w = p * jnp.sum(jnp.where(square, weights[...], 0.0), axis=1, keepdims=True)
         p_hi, w_hi = p.astype(BF16), w.astype(BF16)
         p_lo = (p - p_hi.astype(F32)).astype(BF16)
         w_lo = (w - w_hi.astype(F32)).astype(BF16)
@@ -88,7 +93,7 @@
             ]
             + [
                 pl.BlockSpec((1, count, DEPTH), lambda i, perm, width: (0, 0, i)),
-                pl.BlockSpec((count, 1), lambda i, perm, width: (0, 0)),
+                pl.BlockSpec((1, count), lambda i, perm, width: (0, 0)),
             ],
             out_specs=[
                 pl.BlockSpec((CHUNKS, 8, 4, 2, PART, TILE), lambda i, perm, width: (0,) * 6),
@@ -106,7 +111,7 @@
         ],
         compiler_params=pltpu.CompilerParams(vmem_limit_bytes=48 << 20),
         name="block",
-    )(perm, width, *([coupling] * CLASSES), modes, flexibility.reshape(count, 1))
+    )(perm, width, *([coupling] * CLASSES), modes, flexibility)
 
 
 def exchange_kernel(cap, order, tiles, diag, ring_out, own_out, diag_out, *scratch):
@@ -287,34 +292,35 @@
 
         def add(j, carry, d=d):
             code = place[d, j]
-            tile = own[0, code & 31] if d == 0 else ring[0, d - 1, j]
+            tile = own[:, code & 31] if d == 0 else ring[:, d - 1, j]
             across = pl.ds(pl.multiple_of((code >> 9) * TILE, TILE), TILE)
-            out[(code >> 5) & 15, 0, :, across] += tile
+            out[(code >> 5) & 15, :, :, across] += tile
             return carry
 
         lax.fori_loop(0, count[d], add, 0)
-    inside = pl.ds(pl.multiple_of(chunk * PART, PART), PART)
-    for g in range(ROW_TILES):
-        for h in range(COL_TILES):
-            scale = row_scale[inside, g : g + 1] * col_scale[h : h + 1, :]
-            out[g, 0, :, h * TILE : (h + 1) * TILE] *= scale
-
-
-def assemble(cap, count, place, ring, own, diag, row_hot, col_hot):
+    for part in range(GROUP):
+        inside = pl.ds(pl.multiple_of((chunk * GROUP + part) * PART, PART), PART)
+        for g in range(ROW_TILES):
+            for h in range(COL_TILES):
+                scale = row_scale[inside, g : g + 1] * col_scale[h : h + 1, :]
+                out[g, part, :, h * TILE : (h + 1) * TILE] *= scale
+
+
+def assemble(count, place, ring, own, diag, row_hot, col_hot):
     return pl.pallas_call(
         assemble_kernel,
         grid_spec=pltpu.PrefetchScalarGridSpec(
             num_scalar_prefetch=2,
-            grid=(CHUNKS,),
+            grid=(CHUNKS // GROUP,),
             in_specs=[
-                pl.BlockSpec((1, RING - 1, cap, PART, TILE), lambda q, n, p: (q, 0, 0, 0, 0)),
-                pl.BlockSpec((1, PLANE, PART, TILE), lambda q, n, p: (q, 0, 0, 0)),
+                pl.BlockSpec((GROUP, RING - 1, PLANE, PART, TILE), lambda q, n, p: (q, 0, 0, 0, 0)),
+                pl.BlockSpec((GROUP, PLANE, PART, TILE), lambda q, n, p: (q, 0, 0, 0)),
                 pl.BlockSpec((RING, 2, PLANE, TILE), lambda q, n, p: (0, 0, 0, 0)),
                 pl.BlockSpec((RING * PLANE, 16), lambda q, n, p: (0, 0)),
                 pl.BlockSpec((8, RING * PLANE), lambda q, n, p: (0, 0)),
             ],
             out_specs=pl.BlockSpec(
-                (ROW_TILES, 1, PART, COL_TILES * TILE), lambda q, n, p: (0, q, 0, 0)
+                (ROW_TILES, GROUP, PART, COL_TILES * TILE), lambda q, n, p: (0, q, 0, 0)
             ),
             scratch_shapes=[pltpu.VMEM((TILE, 16), F32), pltpu.VMEM((8, TILE), F32)],
         ),
@@ -368,19 +374,13 @@
 def body(coupling, modes, flexibility, widths, segments):
     row, col = lax.axis_index("row"), lax.axis_index("col")
     perm, order, need, count, place, row_hot, col_hot = places(segments, row, col)
-    tiles, diag = make_block(coupling, modes, flexibility[0], widths, perm)
-
-    def within(cap):
-        def run(order, tiles, diag, count, place, row_hot, col_hot):
-            ring, own, diags = exchange(cap, order, tiles, diag)
-            return assemble(cap, count, place, ring, own, diags, row_hot, col_hot)
-
-        return run
+    tiles, diag = make_block(coupling, modes, flexibility, widths, perm)
 
     level = jnp.sum((need > jnp.array(CAPS[:-1])).astype(jnp.int32))
-    out = lax.switch(
-        level, [within(cap) for cap in CAPS], order, tiles, diag, count, place, row_hot, col_hot
+    ring, own, diags = lax.switch(
+        level, [functools.partial(exchange, cap) for cap in CAPS], order, tiles, diag
     )
+    out = assemble(count, place, ring, own, diags, row_hot, col_hot)
     return out.reshape(ROW_TILES * TILE, COL_TILES * TILE)
 
 

time: 125 us -> 119 us (0.952)
  Pallas kernels: 112 us -> 108 us
  local copies, waits for them, and re-layouts: 5.62 us -> 3.28 us
    pallas_call x1, Pallas kernels: 16.7 us -> 14.7 us  [make_block(): pl.pallas_call(functools.partial(block_kernel, steps), grid_spec=pltpu.Pr...]
    pallas_call x1, Pallas kernels: 9.89 us -> 8.04 us  [assemble(): pl.pallas_call(assemble_kernel, grid_spec=pltpu.PrefetchScalarGridSpec(nu...]
    unnamed x4, local copies, waits for them, and re-layouts: 3.61 us -> 2.1 us
where the time goes in v3:
time: 119 us
  Pallas kernels  108 us (91%)
  other arithmetic  6.1 us (5%)
  local copies, waits for them, and re-layouts  3.28 us (3%)
  between operations  1.55 us (1%)
    pallas_call x1, Pallas kernels, exchange(): pl.pallas_call(functools.partial(exchange_kernel, cap), in_specs=[pl.Bloc...  85.1 us
    pallas_call x1, Pallas kernels, make_block(): pl.pallas_call(functools.partial(block_kernel, steps), grid_spec=pltpu.Pr...  14.7 us
    pallas_call x1, Pallas kernels, assemble(): pl.pallas_call(assemble_kernel, grid_spec=pltpu.PrefetchScalarGridSpec(nu...  8.04 us

profile of v3, /device:TPU:6, one launch (start us, length us, event | category | flops | bytes accessed | tf_op | source)
XLA Modules:
  0.0 118.9 jit_solution(18441540972259240637)
XLA Ops:
  0.0 0.7 broadcast_and_fusion
  0.7 0.8 select_reduce_fusion.4
  1.5 0.1 copy.18
  1.7 0.1 iota_compare_fusion.7
  1.7 0.1 select_reduce_fusion
  1.9 0.6 select_reduce_fusion.2
  2.5 0.2 convert_reduce_fusion.1.count
  2.7 0.1 copy.24
  2.8 0.1 mul.52
  2.9 0.1 copy.23
  3.0 0.1 mul.49
  3.1 0.1 copy.22
  3.2 0.1 iota_compare_fusion.6
  3.3 0.1 select_reduce_fusion.6
  3.4 0.1 bitcast_compare_fusion
  3.4 0.1 copy.20
  3.6 0.1 eq.174
  3.7 0.2 convert_reduce_fusion
  3.9 0.2 select_reduce_fusion.1
  4.2 0.1 broadcast_add_fusion
  4.3 0.6 fusion.3
  4.9 2.0 %fusion.5 = s32[]{:T(128)} fusion(s32[5]{0:T(128)} %constant.65.clone, s32[]{:T(128)} %fusion.3), kind=kLoop, calls=%fused_computation.38 | loop fusion | flops 14 | bytes 28 | tf_op jit(solution)/shard_map/reduce_sum | solution.py:379
  8.3 0.0 copy-start
  8.3 1.4 %copy-done = bf16[1,200,4096]{2,1,0:T(8,128)(2,1)S(1)} copy-done((bf16[1,200,4096]{2,1,0:T(8,128)(2,1)S(1)}, bf16[1,200,4096]{2,1,0:T(8,128)(2,1)}, u32[]{:S(2)}) %copy-start) | copy-done | bytes 1638424
  9.7 0.0 copy-start.1
  9.7 0.7 copy-done.1
  10.4 14.7 %block.1 = (f32[8,8,4,2,16,128]{5,4,3,2,1,0:T(8,128)S(1)}, f32[8,128]{1,0:T(8,128)S(1)}) custom-call(s32[8]{0:T(128)S(1)} %get-tuple-element.71.perm, s32[1]{0:T(128)S(6)} %copy.47.width, bf16[1,4096,1024]{2,1,0:T(8,128)(2,1)} %refs_7_.1, bf16[1,4096,1024]{2,1,0:T(8,128)(2,1)} %refs_7_.1, bf16[1,4096,1024]{2,1,0:T(8,128)(2,1)} %refs_7_.1, ...), custom_call_target="tpu_custom_call" | custom-call | tf_op jit(solution)/shard_map/block/pallas_call | solution.py:86
  25.1 85.2 %conditional.1 = ((f32[8,3,32,16,128]{4,3,2,1,0:T(8,128)}, f32[8,32,16,128]{3,2,1,0:T(8,128)S(1)}, f32[4,2,32,128]{3,2,1,0:T(8,128)S(1)})) conditional(s32[]{:T(128)} %clamp.3, (s32[3,32]{1,0:T(4,128)S(1)}, f32[8,8,4,2,16,128]{5,4,3,2,1,0:T(8,128)S(1)}, f32[8,128]{1,0:T(8,128)S(1)}) %tuple.23, ...), branch_computations={%region_12.13_spmd, %region_13.14_spmd, %region_14.15_spmd, %regio... | conditional | bytes 8 | solution.py:380
  25.2 85.1 %exchange.7 = (f32[8,3,32,16,128]{4,3,2,1,0:T(8,128)}, f32[8,32,16,128]{3,2,1,0:T(8,128)S(1)}, f32[4,2,32,128]{3,2,1,0:T(8,128)S(1)}) custom-call(s32[3,32]{1,0:T(4,128)S(1)} %get-tuple-element.44.order, f32[8,8,4,2,16,128]{5,4,3,2,1,0:T(8,128)S(1)} %get-tuple-element.45.tiles, f32[8,128]{1,0:T(8,128)S(1)} %get-tuple-element.46.diag), custom_call_target="tpu_custom_call" | custom-call | tf_op jit(solution)/shard_map/cond/branch_1_fun/exchange/pallas_call | solution.py:241
  110.3 0.1 copy.26
  110.4 0.1 shift_right_arithmetic.98
  110.5 0.1 fusion.1.row_hot
  110.6 0.1 copy.27
  110.7 0.1 select_n.66
  110.8 8.0 %assemble.1 = f32[12,8,16,768]{3,2,1,0:T(8,128)} custom-call(s32[4]{0:T(128)S(1)} %convert_reduce_fusion.1.count, s32[4,32]{1,0:T(4,128)S(1)} %slice_bitcast_fusion.1.place, f32[8,3,32,16,128]{4,3,2,1,0:T(8,128)} %get-tuple-element.66.ring, f32[8,32,16,128]{3,2,1,0:T(8,128)S(1)} %get-tuple-element.67.own, f32[4,2,32,128]{3,2,1,0:T(8,128)S(1)} %get-tuple-element.68.diag, ...), custom_call_target="tpu_custom_call" | custom-call | tf_op jit(solution)/shard_map/assemble/pallas_call | solution.py:310
  (22 shorter events, 0.2 us)
Async XLA Ops:
  8.3 1.4 %copy-start = (bf16[1,200,4096]{2,1,0:T(8,128)(2,1)S(1)}, bf16[1,200,4096]{2,1,0:T(8,128)(2,1)}, u32[]{:S(2)}) copy-start(bf16[1,200,4096]{2,1,0:T(8,128)(2,1)} %refs_8_.1) | copy-start | bytes 4915204
  9.7 0.7 copy-start.1
